TPU v7x, 256 devices: a whole 4x4x8 slice. The times are simulated.
256 devices in a mesh: gz: 8 (over z_lo, core), gx: 32 (over x, z_hi, y).
Axes of the slice: x: 4, y: 4, z: 8 (z_hi: 2, z_lo: 4; z = z_hi * 4 + z_lo), core: 2. Of those that a mesh axis runs over, the one named last changes fastest.
Arguments:
- state: float32 [6, 128, 8192], P(None, 'gz', 'gx'), may hold values from -5 to 5, as said below
- state_cot: float32 [6, 128, 8192], P(None, 'gz', 'gx'), may hold values from -6 to 6
- w_in: bfloat16 [128, 12], replicated, may hold values from -1.75 to 1.75
- w_mid: bfloat16 [128, 128], replicated, may hold values from -0.5 to 0.5
- w_out: bfloat16 [6, 128], replicated, may hold values from -0.5 to 0.5
- radiation: float32 [128, 128], replicated, may hold values from -0.5 to 0.5
- fall_rate: float32 [8192], P('gx'), may hold values from 20 to 2000
- active: int32 [8192], P('gx'), may hold values 0 or 1
Outputs:
- new_state: float32 [6, 128, 8192], P(None, 'gz', 'gx')
- state_grad: float32 [6, 128, 8192], P(None, 'gz', 'gx')
- grad_in: float32 [128, 12], replicated
- grad_mid: float32 [128, 128], replicated
- grad_out: float32 [6, 128], replicated
Inputs may be any that keep to these rules, and one draw needn't show every extreme that they name: `state`: fields come in the order u, v, w, theta, total water, rain water; rain water lies between 0.05 and 1.
All inputs are finite; a program needn't handle non-finite values. No bound on the sum of `active` on one device may be relied on, other than what follows from the above.
Results may differ from a plain program's by a relative error of at most 0.00045.
The roundings to bfloat16 on the way count: a program that leaves them out, or rounds other values in their place, can miss the bound.
Values sent between devices are 32-bit elements; how exact they have to be, the bound alone decides.
No kernel may reach another device: no remote copies, remote signals or barrier semaphores. Data moves between devices by JAX's collectives and lax.ppermute only.
A program may use at most 64 MiB of HBM per device.

v0:
```python
import jax
import jax.numpy as jnp
from jax import lax
from jax.sharding import PartitionSpec as P

NY = 64
DIFFUSION = 0.1
TIME_STEP = 0.25
CLOSURE_GAIN = 1.0
HEATING_GAIN = 1.0
FALL_GAIN = 1.0


def prefix(shard, axis, combine, identity, reverse):
    length, index = (lax.axis_size(axis), lax.axis_index(axis))
    everything = jax.tree.map(lambda part: lax.all_gather(part, axis), shard)
    start = jax.tree.map(
        lambda part, zero: jnp.broadcast_to(jnp.asarray(zero, part.dtype), part.shape),
        shard,
        identity,
    )

    def step(k, before):
        at = length - 1 - k if reverse else k
        reached = at > index if reverse else at < index
        new = combine(before, jax.tree.map(lambda part: part[at], everything))
        return jax.tree.map(lambda a, b: jnp.where(reached, a, b), new, before)

    return lax.fori_loop(0, length, step, start)


def passed_along(shard, axis, by):
    length = lax.axis_size(axis)
    return lax.ppermute(shard, axis, [(i, (i + by) % length) for i in range(length)])


def padded_2(shard, sides, width):
    for axis, dim in sides:
        size, length = (lax.axis_size(axis), shard.shape[dim])
        up = [(i, (i + 1) % size) for i in range(size)]
        down = [(j, i) for i, j in up]
        last = lax.slice_in_dim(shard, length - width, length, axis=dim)
        first = lax.slice_in_dim(shard, 0, width, axis=dim)
        before = lax.ppermute(last, axis, up)
        after = lax.ppermute(first, axis, down)
        shard = jnp.concatenate([before, shard, after], axis=dim)
    return shard


def contract(left, right, left_dim, right_dim):
    return lax.dot_general(
        left, right, (((left_dim,), (right_dim,)), ((), ())), preferred_element_type=jnp.float32
    )


def mlp_forward(features, w_in, w_mid, w_out):
    hidden_one = jnp.tanh(jnp.dot(w_in, features, preferred_element_type=jnp.float32)).astype(
        jnp.bfloat16
    )
    hidden_two = jnp.tanh(jnp.dot(w_mid, hidden_one, preferred_element_type=jnp.float32)).astype(
        jnp.bfloat16
    )
    return jnp.dot(w_out, hidden_two, preferred_element_type=jnp.float32)


def mlp_backward(features, out_cot, w_in, w_mid, w_out):
    tanh_one = jnp.tanh(jnp.dot(w_in, features, preferred_element_type=jnp.float32))
    hidden_one = tanh_one.astype(jnp.bfloat16)
    tanh_two = jnp.tanh(jnp.dot(w_mid, hidden_one, preferred_element_type=jnp.float32))
    hidden_two = tanh_two.astype(jnp.bfloat16)
    term_out = contract(out_cot, hidden_two, 1, 1)
    pre_two = (contract(w_out, out_cot, 0, 0) * (1.0 - tanh_two * tanh_two)).astype(jnp.bfloat16)
    term_mid = contract(pre_two, hidden_one, 1, 1)
    pre_one = (contract(w_mid, pre_two, 0, 0) * (1.0 - tanh_one * tanh_one)).astype(jnp.bfloat16)
    term_in = contract(pre_one, features, 1, 1)
    feature_cot = contract(w_in, pre_one, 0, 0)
    return (feature_cot, (term_in, term_mid, term_out))


def interior(padded):
    return padded[..., 2 * NY : padded.shape[-1] - 2 * NY]


def dynamics(padded):
    columns = padded.shape[-1] - 4 * NY

    def along_x(offset):
        first_col = 2 * NY + offset * NY
        return padded[..., first_col : first_col + columns]

    center = along_x(0)
    y_place = jnp.arange(columns) % NY
    y_last = y_place == NY - 1
    y_first = y_place == 0
    y_plus = jnp.where(y_last, jnp.roll(center, NY - 1, -1), jnp.roll(center, -1, -1))
    y_minus = jnp.where(y_first, jnp.roll(center, 1 - NY, -1), jnp.roll(center, 1, -1))
    x_plus, x_minus = (along_x(1), along_x(-1))
    deriv_x = (8.0 * (x_plus - x_minus) - (along_x(2) - along_x(-2))) / 12.0
    deriv_y = (y_plus - y_minus) / 2.0
    laplace = x_plus + x_minus + y_plus + y_minus - 4.0 * center
    return (-(center[0] * deriv_x + center[1] * deriv_y) + DIFFUSION * laplace, deriv_x)


def compose(earlier, later):
    return (later[0] * earlier[0], later[1] + later[0] * earlier[1])


def running_maps(source, retained):
    factors = jnp.broadcast_to(retained, source.shape)
    return lax.associative_scan(compose, (factors, source), axis=0)


def sediment_forward(rain_water, fall_speed):
    fresh_share = 1.0 / (1.0 + fall_speed)
    retained = fall_speed / (1.0 + fall_speed)
    factors, values = running_maps(jnp.flip(fresh_share * rain_water, 0), retained)
    inflow = prefix(
        (factors[-1], values[-1]),
        "gz",
        compose,
        (jnp.ones_like(fall_speed), jnp.zeros_like(fall_speed)),
        True,
    )
    return jnp.flip(values + factors * inflow[1], 0)


def sediment_adjoint(source, fall_speed):
    fresh_share = 1.0 / (1.0 + fall_speed)
    retained = fall_speed / (1.0 + fall_speed)
    factors, values = running_maps(fresh_share * source, retained)
    inflow = prefix(
        (factors[-1], values[-1]),
        "gz",
        compose,
        (jnp.ones_like(fall_speed), jnp.zeros_like(fall_speed)),
        False,
    )
    return values + factors * inflow[1]


def heating(theta, radiation):
    levels = theta.shape[0]
    own_rows = lax.dynamic_slice_in_dim(radiation, lax.axis_index("gz") * levels, levels, 0)
    return jnp.dot(
        own_rows,
        lax.all_gather(theta, "gz", axis=0, tiled=True),
        precision=lax.Precision.HIGHEST,
        preferred_element_type=jnp.float32,
    )


def heating_adjoint(lead_theta, radiation):
    levels = lead_theta.shape[0]
    own_rows = lax.dynamic_slice_in_dim(radiation, lax.axis_index("gz") * levels, levels, 0)
    return lax.psum_scatter(
        lax.dot_general(
            own_rows,
            lead_theta,
            (((0,), (0,)), ((), ())),
            precision=lax.Precision.HIGHEST,
            preferred_element_type=jnp.float32,
        ),
        "gz",
        scatter_dimension=0,
        tiled=True,
    )


def tendency(padded, w_in, w_mid, w_out, radiation, fall_speed, live):
    moved, deriv_x = dynamics(padded)
    center = interior(padded)
    fields, levels, columns = center.shape
    features = (
        jnp.concatenate([center, deriv_x], 0)
        .astype(jnp.bfloat16)
        .reshape(2 * fields, levels * columns)
    )
    closure = mlp_forward(features, w_in, w_mid, w_out).reshape(fields, levels, columns)
    total = moved + CLOSURE_GAIN * closure
    total = total.at[3].add(HEATING_GAIN * heating(center[3], radiation))
    fallen = sediment_forward(center[5], fall_speed)
    return total.at[5].add(FALL_GAIN * live * (fallen - center[5]))


def adjoint_tendency(padded, lead, w_in, w_mid, w_out, radiation, fall_speed, live):
    outputs, pullback = jax.vjp(dynamics, padded)
    center = interior(padded)
    fields, levels, columns = center.shape
    features = (
        jnp.concatenate([center, outputs[1]], 0)
        .astype(jnp.bfloat16)
        .reshape(2 * fields, levels * columns)
    )
    out_cot = (CLOSURE_GAIN * lead).astype(jnp.bfloat16).reshape(fields, levels * columns)
    feature_cot, grads = mlp_backward(features, out_cot, w_in, w_mid, w_out)
    feature_cot = feature_cot.reshape(2 * fields, levels, columns)
    padded_cot = pullback((lead, feature_cot[fields:]))[0]
    rim_width = 2 * NY
    from_next = passed_along(padded_cot[..., :rim_width], "gx", -1)
    from_prev = passed_along(padded_cot[..., padded_cot.shape[-1] - rim_width :], "gx", 1)
    result = interior(padded_cot) + feature_cot[:fields]
    result = result.at[..., :rim_width].add(from_prev)
    result = result.at[..., columns - rim_width :].add(from_next)
    result = result.at[3].add(HEATING_GAIN * heating_adjoint(lead[3], radiation))
    masked = live * lead[5]
    return (result.at[5].add(FALL_GAIN * (sediment_adjoint(masked, fall_speed) - masked)), grads)


def on_device(state, state_cot, w_in, w_mid, w_out, radiation, fall_rate, active):
    live = active.astype(jnp.float32)

    def extend(fields):
        return padded_2(fields, (("gx", 2),), 2 * NY)

    def section_tendency(padded):
        return tendency(padded, w_in, w_mid, w_out, radiation, fall_rate, live)

    def section_adjoint(padded, lead):
        return adjoint_tendency(padded, lead, w_in, w_mid, w_out, radiation, fall_rate, live)

    padded_zero = extend(state)
    section_one = state + TIME_STEP * section_tendency(padded_zero)
    padded_one = extend(section_one)
    section_two = 0.75 * state + 0.25 * (section_one + TIME_STEP * section_tendency(padded_one))
    padded_two = extend(section_two)
    new_state = state / 3.0 + 2.0 / 3.0 * (section_two + TIME_STEP * section_tendency(padded_two))
    lead_two = 2.0 / 3.0 * state_cot
    grad_state = state_cot / 3.0
    back_two, grads_two = section_adjoint(padded_two, lead_two)
    cot_two = lead_two + TIME_STEP * back_two
    lead_one = 0.25 * cot_two
    grad_state = grad_state + 0.75 * cot_two
    back_one, grads_one = section_adjoint(padded_one, lead_one)
    cot_one = lead_one + TIME_STEP * back_one
    back_zero, grads_zero = section_adjoint(padded_zero, cot_one)
    grad_state = grad_state + cot_one + TIME_STEP * back_zero
    totals = lax.psum(
        (
            TIME_STEP * (grads_two[0] + grads_one[0] + grads_zero[0]),
            TIME_STEP * (grads_two[1] + grads_one[1] + grads_zero[1]),
            TIME_STEP * (grads_two[2] + grads_one[2] + grads_zero[2]),
        ),
        ("gz", "gx"),
    )
    return (new_state, grad_state, totals[0], totals[1], totals[2])


def solution(mesh):
    placed = (P(None, "gz", "gx"), P(None, "gz", "gx"), P(), P(), P(), P(), P("gx"), P("gx"))
    return jax.shard_map(
        on_device,
        mesh=mesh,
        in_specs=placed,
        out_specs=(P(None, "gz", "gx"), P(None, "gz", "gx"), P(), P(), P()),
        check_vma=False,
    )
```

profile of v0, /device:TPU:1, one launch (start us, length us, event | category | flops | bytes accessed | tf_op | source)
XLA Modules:
  0.0 674.6 jit_solution(1791743276329991955)
XLA Ops:
  8.1 12.5 %collective-permute-start = (f32[6,16,128]{2,1,0:T(8,128)S(1)}, f32[6,16,128]{2,1,0:T(8,128)S(1)}, u32[]{:S(2)}, u32[]{:S(2)}) collective-permute-start(f32[6,16,128]{2,1,0:T(8,128)S(1)} %get-tuple-element.1230), channel_id=1, source_target_pairs={{1,0},{2,1},{3,2},{4,3},{5,4},{6,5},{7,6},{8,7},{9,8},{10,9},{11,1... | collective-permute-start | bytes 147464 | tf_op jit(solution)/shard_map/ppermute | solution.py:45
  21.9 1.4 bitcast_multiply_fusion
  23.6 1.5 fusion.147
  25.2 1.5 fusion.146
  27.7 1.6 fusion.145
  30.5 11.1 %all-gather.3 = f32[8,1,256]{2,1,0:T(1,128)S(1)} all-gather(f32[1,1,256]{2,1,0:T(1,128)S(1)} %add_bitcast_fusion.6), channel_id=1, replica_groups=mesh['gz'=8,'gx'=32] {'gz'}, dimensions={0}, use_global_device_ids=true | all-gather | bytes 9216 | tf_op jit(solution)/shard_map/all_gather | solution.py:16
  41.6 8.7 %all-gather.4 = f32[8,1,256]{2,1,0:T(1,128)S(1)} all-gather(f32[1,1,256]{2,1,0:T(1,128)S(1)} %add_bitcast_fusion.5), channel_id=1, replica_groups=mesh['gz'=8,'gx'=32] {'gz'}, dimensions={0}, use_global_device_ids=true | all-gather | bytes 9216 | tf_op jit(solution)/shard_map/all_gather | solution.py:16
  51.5 14.0 %all-gather = f32[1,128,256]{2,1,0:T(8,128)S(1)} all-gather(f32[1,16,256]{2,1,0:T(8,128)S(1)} %slice-done), channel_id=2, replica_groups=mesh['gz'=8,'gx'=32] {'gz'}, dimensions={1}, use_global_device_ids=true | all-gather | bytes 147456 | tf_op jit(solution)/shard_map/all_gather | solution.py:146
  73.2 10.1 %all-gather.5 = f32[8,1,256]{2,1,0:T(1,128)S(1)} all-gather(f32[1,1,256]{2,1,0:T(1,128)S(1)} %add_bitcast_fusion.4), channel_id=1, replica_groups=mesh['gz'=8,'gx'=32] {'gz'}, dimensions={0}, use_global_device_ids=true | all-gather | bytes 9216 | tf_op jit(solution)/shard_map/all_gather | solution.py:16
  83.8 9.9 %collective-permute-start.2 = (f32[6,16,128]{2,1,0:T(8,128)S(1)}, f32[6,16,128]{2,1,0:T(8,128)S(1)}, u32[]{:S(2)}, u32[]{:S(2)}) collective-permute-start(f32[6,16,128]{2,1,0:T(8,128)S(1)} %get-tuple-element.1214), channel_id=1, source_target_pairs={{1,0},{2,1},{3,2},{4,3},{5,4},{6,5},{7,6},{8,7},{9,8},{10,9},{11,1... | collective-permute-start | bytes 147464 | tf_op jit(solution)/shard_map/ppermute | solution.py:45
  93.8 14.3 %all-gather.1 = f32[1,128,256]{2,1,0:T(8,128)S(1)} all-gather(f32[1,16,256]{2,1,0:T(8,128)S(1)} %get-tuple-element.1172), channel_id=3, replica_groups=mesh['gz'=8,'gx'=32] {'gz'}, dimensions={1}, use_global_device_ids=true | all-gather | bytes 147456 | tf_op jit(solution)/shard_map/all_gather | solution.py:146
  113.3 9.9 %collective-permute-start.4 = (f32[6,16,128]{2,1,0:T(8,128)S(1)}, f32[6,16,128]{2,1,0:T(8,128)S(1)}, u32[]{:S(2)}, u32[]{:S(2)}) collective-permute-start(f32[6,16,128]{2,1,0:T(8,128)S(1)} %get-tuple-element.1193), channel_id=1, source_target_pairs={{1,0},{2,1},{3,2},{4,3},{5,4},{6,5},{7,6},{8,7},{9,8},{10,9},{11,1... | collective-permute-start | bytes 147464 | tf_op jit(solution)/shard_map/ppermute | solution.py:45
  123.2 15.5 %all-gather.2 = f32[1,128,256]{2,1,0:T(8,128)} all-gather(f32[1,16,256]{2,1,0:T(8,128)S(1)} %get-tuple-element.1188), channel_id=4, replica_groups=mesh['gz'=8,'gx'=32] {'gz'}, dimensions={1}, use_global_device_ids=true | all-gather | bytes 147456 | tf_op jit(solution)/shard_map/all_gather | solution.py:146
  138.7 1.5 broadcast_multiply_fusion
  153.3 8.7 %all-gather.7 = f32[8,1,256]{2,1,0:T(1,128)S(1)} all-gather(f32[1,1,256]{2,1,0:T(1,128)S(1)} %add_bitcast_fusion.2), channel_id=1, replica_groups=mesh['gz'=8,'gx'=32] {'gz'}, dimensions={0}, use_global_device_ids=true | all-gather | bytes 9216 | tf_op jit(solution)/shard_map/all_gather | solution.py:16
  162.1 8.8 %while.111 = (s32[]{:T(128)}, f32[256]{0:T(256)}, s32[]{:T(128)}, f32[8,256]{1,0:T(8,128)S(1)}, f32[8,256]{1,0:T(8,128)S(1)}, /*index=5*/s32[]{:T(128)}, s32[]{:T(128)}) while((s32[]{:T(128)}, f32[256]{0:T(256)}, s32[]{:T(128)}, f32[8,256]{1,0:T(8,128)S(1)}, f32[8,256]{1,0:T(8,128)S(1)}, /*index=5*/s32[]{:T(128)}, ...), condition=%wide.region_10.11_spmd.clone, body=%wide.region_9.10_spmd.clone.sunk | while | flops 1028 | bytes 8301 | solution.py:29
  170.9 9.9 %collective-permute-start.7 = (f32[6,16,128]{2,1,0:T(8,128)S(1)}, f32[6,16,128]{2,1,0:T(8,128)S(1)}, u32[]{:S(2)}, u32[]{:S(2)}) collective-permute-start(f32[6,16,128]{2,1,0:T(8,128)S(1)} %get-tuple-element.1127), channel_id=1, source_target_pairs={{0,31},{1,0},{2,1},{3,2},{4,3},{5,4},{6,5},{7,6},{8,7},{9,8},{10,9... | collective-permute-start | bytes 147464 | tf_op jit(solution)/shard_map/ppermute | solution.py:34
  180.9 11.1 %collective-permute-done.6 = f32[6,16,128]{2,1,0:T(8,128)S(1)} collective-permute-done((f32[6,16,128]{2,1,0:T(8,128)S(1)}, f32[6,16,128]{2,1,0:T(8,128)S(1)}, u32[]{:S(2)}, u32[]{:S(2)}) %collective-permute-start.6) | collective-permute-done | bytes 49184 | tf_op jit(solution)/shard_map/ppermute | solution.py:34
  192.0 12.1 %reduce-scatter.4.cloned.1.call-done = f32[16,256]{1,0:T(8,128)} async-done(((f32[128,256]{1,0:T(8,128)}), f32[16,256]{1,0:T(8,128)}) %reduce-scatter.4.cloned.1.call-update) | async-done | bytes 16400 | tf_op jit(solution)/shard_map/reduce_scatter | solution.py:155
  211.1 2.2 fusion.2
  218.2 1.8 pad.467
  220.1 1.9 pad.468
  221.9 1.3 add.1082
  225.2 1.9 pad.470
  227.0 1.3 add.1084
  230.4 1.9 pad.472
  233.0 12.0 %all-gather.8 = f32[8,1,256]{2,1,0:T(1,128)S(1)} all-gather(f32[1,1,256]{2,1,0:T(1,128)S(1)} %add_bitcast_fusion.1), channel_id=1, replica_groups=mesh['gz'=8,'gx'=32] {'gz'}, dimensions={0}, use_global_device_ids=true | all-gather | bytes 9216 | tf_op jit(solution)/shard_map/all_gather | solution.py:16
  245.6 15.3 %while.112 = (s32[]{:T(128)}, f32[256]{0:T(256)}, s32[]{:T(128)}, f32[8,256]{1,0:T(8,128)}, f32[8,256]{1,0:T(8,128)}, /*index=5*/s32[]{:T(128)}, s32[]{:T(128)}) while((s32[]{:T(128)}, f32[256]{0:T(256)}, s32[]{:T(128)}, f32[8,256]{1,0:T(8,128)}, f32[8,256]{1,0:T(8,128)}, /*index=5*/s32[]{:T(128)}, s32[]{:T(128)}) %tuple.457), condition=%wide.region_15.16_spmd.clone, body=%wide.region_14.15_spmd.clone.sunk | while | flops 1028 | bytes 8301 | solution.py:29
  260.9 2.6 convolution_add_fusion.5
  263.5 2.4 convolution_add_fusion.1
  266.9 7.8 %collective-permute-start.9 = (f32[6,16,128]{2,1,0:T(8,128)}, f32[6,16,128]{2,1,0:T(8,128)S(1)}, u32[]{:S(2)}, u32[]{:S(2)}) collective-permute-start(f32[6,16,128]{2,1,0:T(8,128)} %get-tuple-element.1125), channel_id=1, source_target_pairs={{0,31},{1,0},{2,1},{3,2},{4,3},{5,4},{6,5},{7,6},{8,7},{9,8},{10,9... | collective-permute-start | bytes 147464 | tf_op jit(solution)/shard_map/ppermute | solution.py:34
  275.7 10.3 %collective-permute-done.8 = f32[6,16,128]{2,1,0:T(8,128)S(1)} collective-permute-done((f32[6,16,128]{2,1,0:T(8,128)}, f32[6,16,128]{2,1,0:T(8,128)S(1)}, u32[]{:S(2)}, u32[]{:S(2)}) %collective-permute-start.8) | collective-permute-done | bytes 49184 | tf_op jit(solution)/shard_map/ppermute | solution.py:34
  286.1 12.3 %reduce-scatter.6.cloned.1.call-done = f32[16,256]{1,0:T(8,128)} async-done(((f32[128,256]{1,0:T(8,128)}), f32[16,256]{1,0:T(8,128)}) %reduce-scatter.6.cloned.1.call-update) | async-done | bytes 16400 | tf_op jit(solution)/shard_map/reduce_scatter | solution.py:155
  299.9 1.6 multiply_reduce_fusion.1
  328.3 1.3 add.1046
  330.2 1.3 fusion.92
  332.1 1.3 pad_maximum_fusion.19
  334.2 1.9 pad.495
  336.8 12.1 %all-gather.9 = f32[8,1,256]{2,1,0:T(1,128)S(1)} all-gather(f32[1,1,256]{2,1,0:T(1,128)S(1)} %add_bitcast_fusion), channel_id=1, replica_groups=mesh['gz'=8,'gx'=32] {'gz'}, dimensions={0}, use_global_device_ids=true | all-gather | bytes 9216 | tf_op jit(solution)/shard_map/all_gather | solution.py:16
  349.4 14.0 %while.113 = (s32[]{:T(128)}, f32[256]{0:T(256)}, s32[]{:T(128)}, f32[8,256]{1,0:T(8,128)}, f32[8,256]{1,0:T(8,128)}, /*index=5*/s32[]{:T(128)}, s32[]{:T(128)}) while((s32[]{:T(128)}, f32[256]{0:T(256)}, s32[]{:T(128)}, f32[8,256]{1,0:T(8,128)}, f32[8,256]{1,0:T(8,128)}, /*index=5*/s32[]{:T(128)}, s32[]{:T(128)}) %tuple.458), condition=%wide.region_20.21_spmd.clone, body=%wide.region_19.20_spmd.clone.sunk | while | flops 1028 | bytes 8301 | solution.py:29
  364.2 10.4 %all-gather.6 = f32[8,1,256]{2,1,0:T(1,128)S(1)} all-gather(f32[1,1,256]{2,1,0:T(1,128)S(1)} %add_bitcast_fusion.3), channel_id=1, replica_groups=mesh['gz'=8,'gx'=32] {'gz'}, dimensions={0}, use_global_device_ids=true | all-gather | bytes 9216 | tf_op jit(solution)/shard_map/all_gather | solution.py:16
  375.1 14.2 %while.110 = (s32[]{:T(128)}, f32[256]{0:T(256)}, s32[]{:T(128)}, f32[8,256]{1,0:T(8,128)}, f32[8,256]{1,0:T(8,128)}, /*index=5*/s32[]{:T(128)}, s32[]{:T(128)}, s32[]{:T(128)}, s32[]{:T(128)}) while((s32[]{:T(128)}, f32[256]{0:T(256)}, s32[]{:T(128)}, f32[8,256]{1,0:T(8,128)}, f32[8,256]{1,0:T(8,128)}, /*index=5*/s32[]{:T(128)}, ...), condition=%wide.region_5.6_spmd.clone, body=%wide.region_4.5_spmd.clone.sunk | while | flops 1032 | bytes 8363 | solution.py:29
  389.5 1.8 fusion.14
  391.5 2.5 fusion.6
  395.7 8.6 %collective-permute-start.11 = (f32[6,16,128]{2,1,0:T(8,128)S(1)}, f32[6,16,128]{2,1,0:T(8,128)S(1)}, u32[]{:S(2)}, u32[]{:S(2)}) collective-permute-start(f32[6,16,128]{2,1,0:T(8,128)S(1)} %copy-done.103), channel_id=1, source_target_pairs={{0,31},{1,0},{2,1},{3,2},{4,3},{5,4},{6,5},{7,6},{8,7},{9,8},{10,9... | collective-permute-start | bytes 147464 | tf_op jit(solution)/shard_map/ppermute | solution.py:34
  404.7 73.1 %all-reduce.101 = (f32[128,12]{0,1:T(8,128)}, f32[6,128]{1,0:T(8,128)}) all-reduce(f32[128,12]{0,1:T(8,128)S(1)} %fusion.13, f32[6,128]{1,0:T(8,128)S(1)} %copy-done.124), channel_id=1, replica_groups=mesh['gz'=8,'gx'=32] {'gz','gx'}, use_global_device_ids=true, to_apply=%region_21.22 | all-reduce | flops 2304 | bytes 18432 | tf_op jit(solution)/shard_map/psum | solution.py:237
  480.0 186.6 %all-reduce.104.cloned.1.call-done = f32[128,128]{1,0:T(8,128)} async-done(((f32[128,128]{1,0:T(8,128)}), f32[128,128]{1,0:T(8,128)}) %all-reduce.104.cloned.1.call-update) | async-done | bytes 65552 | tf_op jit(solution)/shard_map/psum | solution.py:237
  666.6 1.5 copy.127
  (725 shorter events, 139.6 us)
Async XLA Ops:
  7.2 62.3 %copy-start = (f32[128,128]{1,0:T(8,128)S(1)}, f32[128,128]{1,0:T(8,128)}, u32[]{:S(2)}) copy-start(f32[128,128]{1,0:T(8,128)} %param.61) | copy-start | bytes 196612
  7.2 44.3 %slice-start = ((f32[6,16,256]{2,1,0:T(8,128)}), f32[1,16,256]{2,1,0:T(8,128)S(1)}, s32[]{:S(2)}) async-start(f32[6,16,256]{2,1,0:T(8,128)} %param.56), calls=%async_computation.7 | async-start | bytes 32768 | tf_op jit(solution)/shard_map/slice | solution.py:180
  7.2 58.3 %copy-start.8 = (f32[6,16,256]{2,1,0:T(8,128)S(1)}, f32[6,16,256]{2,1,0:T(8,128)}, u32[]{:S(2)}) copy-start(f32[6,16,256]{2,1,0:T(8,128)} %param.56) | copy-start | bytes 294916
  7.2 58.5 %copy-start.63 = (bf16[128,12]{0,1:T(8,128)(2,1)S(1)}, bf16[128,12]{0,1:T(8,128)(2,1)}, u32[]{:S(2)}) copy-start(bf16[128,12]{0,1:T(8,128)(2,1)} %param.58) | copy-start | bytes 9220
  7.2 196.9 %reduce-scatter.4.cloned.1.call-start = ((), (), s32[]{:S(2)}) async-start(), calls=%async_computation.3 | async-start | bytes 147456 | tf_op jit(solution)/shard_map/reduce_scatter | solution.py:155
  8.1 57.4 %collective-permute-start = (f32[6,16,128]{2,1,0:T(8,128)S(1)}, f32[6,16,128]{2,1,0:T(8,128)S(1)}, u32[]{:S(2)}, u32[]{:S(2)}) collective-permute-start(f32[6,16,128]{2,1,0:T(8,128)S(1)} %get-tuple-element.1230), channel_id=1, source_target_pairs={{1,0},{2,1},{3,2},{4,3},{5,4},{6,5},{7,6},{8,7},{9,8},{10,9},{11,1... | collective-permute-start | bytes 147464 | tf_op jit(solution)/shard_map/ppermute | solution.py:45
  20.6 44.9 %collective-permute-start.1 = (f32[6,16,128]{2,1,0:T(8,128)S(1)}, f32[6,16,128]{2,1,0:T(8,128)S(1)}, u32[]{:S(2)}, u32[]{:S(2)}) collective-permute-start(f32[6,16,128]{2,1,0:T(8,128)S(1)} %get-tuple-element.1231), channel_id=1, source_target_pairs={{0,1},{1,2},{2,3},{3,4},{4,5},{5,6},{6,7},{7,8},{8,9},{9,10},{10,1... | collective-permute-start | bytes 147464 | tf_op jit(solution)/shard_map/ppermute | solution.py:44
  21.9 119.7 %copy-start.66 = (f32[256]{0:T(256)}, f32[256]{0:T(256)S(1)}, u32[]{:S(2)}) copy-start(f32[256]{0:T(256)S(1)} %get-tuple-element.1104) | copy-start | bytes 3076
  21.9 130.7 %copy-start.60 = (f32[256]{0:T(256)}, f32[256]{0:T(256)S(1)}, u32[]{:S(2)}) copy-start(f32[256]{0:T(256)S(1)} %get-tuple-element.1105) | copy-start | bytes 3076
  23.3 118.3 %copy-start.47 = (f32[256]{0:T(256)}, f32[256]{0:T(256)S(1)}, u32[]{:S(2)}) copy-start(f32[256]{0:T(256)S(1)} %get-tuple-element.1275) | copy-start | bytes 3076
  30.0 110.2 %copy-start.71 = (f32[256]{0:T(256)}, f32[256]{0:T(256)S(1)}, u32[]{:S(2)}) copy-start(f32[256]{0:T(256)S(1)} %convert_element_type.59) | copy-start | bytes 3076
  50.3 15.9 %copy-start.16 = (bf16[128,128]{1,0:T(8,128)(2,1)S(1)}, bf16[128,128]{1,0:T(8,128)(2,1)}, u32[]{:S(2)}) copy-start(bf16[128,128]{1,0:T(8,128)(2,1)} %param.59) | copy-start | bytes 98308
  50.8 154.0 %copy-start.32 = (f32[16,256]{1,0:T(8,128)}, f32[16,256]{1,0:T(8,128)S(1)}, u32[]{:S(2)}) copy-start(f32[16,256]{1,0:T(8,128)S(1)} %get-tuple-element.1103) | copy-start | bytes 49156
  72.9 36.3 %copy-start.26 = (bf16[1,6,16,256]{3,1,2,0:T(8,128)(2,1)}, bf16[1,6,16,256]{3,1,2,0:T(8,128)(2,1)S(1)}, u32[]{:S(2)}) copy-start(bf16[1,6,16,256]{3,1,2,0:T(8,128)(2,1)S(1)} %copy.23) | copy-start | bytes 147460
  83.8 24.2 %collective-permute-start.2 = (f32[6,16,128]{2,1,0:T(8,128)S(1)}, f32[6,16,128]{2,1,0:T(8,128)S(1)}, u32[]{:S(2)}, u32[]{:S(2)}) collective-permute-start(f32[6,16,128]{2,1,0:T(8,128)S(1)} %get-tuple-element.1214), channel_id=1, source_target_pairs={{1,0},{2,1},{3,2},{4,3},{5,4},{6,5},{7,6},{8,7},{9,8},{10,9},{11,1... | collective-permute-start | bytes 147464 | tf_op jit(solution)/shard_map/ppermute | solution.py:45
  93.8 14.3 %collective-permute-start.3 = (f32[6,16,128]{2,1,0:T(8,128)S(1)}, f32[6,16,128]{2,1,0:T(8,128)S(1)}, u32[]{:S(2)}, u32[]{:S(2)}) collective-permute-start(f32[6,16,128]{2,1,0:T(8,128)S(1)} %get-tuple-element.1215), channel_id=1, source_target_pairs={{0,1},{1,2},{2,3},{3,4},{4,5},{5,6},{6,7},{7,8},{8,9},{9,10},{10,1... | collective-permute-start | bytes 147464 | tf_op jit(solution)/shard_map/ppermute | solution.py:44
  110.6 28.1 %copy-start.11 = (f32[6,16,256]{2,1,0:T(8,128)S(1)}, f32[6,16,256]{2,1,0:T(8,128)}, u32[]{:S(2)}) copy-start(f32[6,16,256]{2,1,0:T(8,128)} %param.57) | copy-start | bytes 294916
  112.0 28.2 %copy-start.107 = (f32[256]{0:T(256)S(1)}, f32[256]{0:T(256)}, u32[]{:S(2)}) copy-start(f32[256]{0:T(256)} %copy-done.105) | copy-start | bytes 3076
  112.0 29.6 %copy-start.94 = (f32[256]{0:T(256)S(1)}, f32[256]{0:T(256)}, u32[]{:S(2)}) copy-start(f32[256]{0:T(256)} %copy-done.92) | copy-start | bytes 3076
  113.3 25.4 %collective-permute-start.4 = (f32[6,16,128]{2,1,0:T(8,128)S(1)}, f32[6,16,128]{2,1,0:T(8,128)S(1)}, u32[]{:S(2)}, u32[]{:S(2)}) collective-permute-start(f32[6,16,128]{2,1,0:T(8,128)S(1)} %get-tuple-element.1193), channel_id=1, source_target_pairs={{1,0},{2,1},{3,2},{4,3},{5,4},{6,5},{7,6},{8,7},{9,8},{10,9},{11,1... | collective-permute-start | bytes 147464 | tf_op jit(solution)/shard_map/ppermute | solution.py:45
  123.2 15.5 %collective-permute-start.5 = (f32[6,16,128]{2,1,0:T(8,128)S(1)}, f32[6,16,128]{2,1,0:T(8,128)S(1)}, u32[]{:S(2)}, u32[]{:S(2)}) collective-permute-start(f32[6,16,128]{2,1,0:T(8,128)S(1)} %get-tuple-element.1194), channel_id=1, source_target_pairs={{0,1},{1,2},{2,3},{3,4},{4,5},{5,6},{6,7},{7,8},{8,9},{9,10},{10,1... | collective-permute-start | bytes 147464 | tf_op jit(solution)/shard_map/ppermute | solution.py:44
  150.4 54.4 %copy-start.72 = (f32[256]{0:T(256)S(1)}, f32[256]{0:T(256)}, u32[]{:S(2)}) copy-start(f32[256]{0:T(256)} %copy-done.71) | copy-start | bytes 3076
  150.7 57.6 %copy-start.48 = (f32[256]{0:T(256)S(1)}, f32[256]{0:T(256)}, u32[]{:S(2)}) copy-start(f32[256]{0:T(256)} %copy-done.47) | copy-start | bytes 3076
  150.9 57.4 %copy-start.95 = (f32[256]{0:T(256)S(1)}, f32[256]{0:T(256)}, u32[]{:S(2)}) copy-start(f32[256]{0:T(256)} %copy-done.92) | copy-start | bytes 3076
  150.9 60.2 %copy-start.75 = (bf16[6,128]{1,0:T(8,128)(2,1)S(1)}, bf16[6,128]{1,0:T(8,128)(2,1)}, u32[]{:S(2)}) copy-start(bf16[6,128]{1,0:T(8,128)(2,1)} %param.60) | copy-start | bytes 4612
  170.9 34.0 %copy-start.59 = (f32[8,256]{1,0:T(8,128)}, f32[8,256]{1,0:T(8,128)S(1)}, u32[]{:S(2)}) copy-start(f32[8,256]{1,0:T(8,128)S(1)} %get-tuple-element.1659) | copy-start | bytes 24580
  170.9 127.5 %reduce-scatter.6.cloned.1.call-start = ((), (), s32[]{:S(2)}) async-start(), calls=%async_computation.4 | async-start | bytes 147456 | tf_op jit(solution)/shard_map/reduce_scatter | solution.py:155
  170.9 21.1 %collective-permute-start.7 = (f32[6,16,128]{2,1,0:T(8,128)S(1)}, f32[6,16,128]{2,1,0:T(8,128)S(1)}, u32[]{:S(2)}, u32[]{:S(2)}) collective-permute-start(f32[6,16,128]{2,1,0:T(8,128)S(1)} %get-tuple-element.1127), channel_id=1, source_target_pairs={{0,31},{1,0},{2,1},{3,2},{4,3},{5,4},{6,5},{7,6},{8,7},{9,8},{10,9... | collective-permute-start | bytes 147464 | tf_op jit(solution)/shard_map/ppermute | solution.py:34
  180.9 11.1 %collective-permute-start.6 = (f32[6,16,128]{2,1,0:T(8,128)S(1)}, f32[6,16,128]{2,1,0:T(8,128)S(1)}, u32[]{:S(2)}, u32[]{:S(2)}) collective-permute-start(f32[6,16,128]{2,1,0:T(8,128)S(1)} %get-tuple-element.1128), channel_id=1, source_target_pairs={{0,1},{1,2},{2,3},{3,4},{4,5},{5,6},{6,7},{7,8},{8,9},{9,10},{10,1... | collective-permute-start | bytes 147464 | tf_op jit(solution)/shard_map/ppermute | solution.py:34
  230.4 30.5 %copy-start.77 = (f32[16,256]{1,0:T(8,128)}, f32[16,256]{1,0:T(8,128)S(1)}, u32[]{:S(2)}) copy-start(f32[16,256]{1,0:T(8,128)S(1)} %pad.471) | copy-start | bytes 49156
  263.5 35.6 %copy-start.33 = (f32[16,256]{1,0:T(8,128)S(1)}, f32[16,256]{1,0:T(8,128)}, u32[]{:S(2)}) copy-start(f32[16,256]{1,0:T(8,128)} %copy-done.32) | copy-start | bytes 49156
  266.8 48.6 %copy-start.96 = (f32[16,256]{1,0:T(8,128)S(1)}, f32[16,256]{1,0:T(8,128)}, u32[]{:S(2)}) copy-start(f32[16,256]{1,0:T(8,128)} %get-tuple-element.1162) | copy-start | bytes 49156
  266.8 48.6 %copy-start.118 = (pred[256]{0:T(512)(128)(4,1)S(1)}, pred[256]{0:T(512)(128)(4,1)}, u32[]{:S(2)}) copy-start(pred[256]{0:T(512)(128)(4,1)} %get-tuple-element.1278) | copy-start | bytes 772
  266.8 48.6 %copy-start.123 = (pred[256]{0:T(512)(128)(4,1)S(1)}, pred[256]{0:T(512)(128)(4,1)}, u32[]{:S(2)}) copy-start(pred[256]{0:T(512)(128)(4,1)} %get-tuple-element.1279) | copy-start | bytes 772
  266.8 49.6 %copy-start.76 = (bf16[6,128]{1,0:T(8,128)(2,1)S(1)}, bf16[6,128]{1,0:T(8,128)(2,1)}, u32[]{:S(2)}) copy-start(bf16[6,128]{1,0:T(8,128)(2,1)} %param.60) | copy-start | bytes 4612
  266.8 211.0 %reduce-scatter.8.cloned.1.call-start = ((), (), s32[]{:S(2)}) async-start(), calls=%async_computation.5 | async-start | bytes 147456 | tf_op jit(solution)/shard_map/reduce_scatter | solution.py:155
  266.9 19.2 %collective-permute-start.9 = (f32[6,16,128]{2,1,0:T(8,128)}, f32[6,16,128]{2,1,0:T(8,128)S(1)}, u32[]{:S(2)}, u32[]{:S(2)}) collective-permute-start(f32[6,16,128]{2,1,0:T(8,128)} %get-tuple-element.1125), channel_id=1, source_target_pairs={{0,31},{1,0},{2,1},{3,2},{4,3},{5,4},{6,5},{7,6},{8,7},{9,8},{10,9... | collective-permute-start | bytes 147464 | tf_op jit(solution)/shard_map/ppermute | solution.py:34
  274.7 11.3 %collective-permute-start.8 = (f32[6,16,128]{2,1,0:T(8,128)}, f32[6,16,128]{2,1,0:T(8,128)S(1)}, u32[]{:S(2)}, u32[]{:S(2)}) collective-permute-start(f32[6,16,128]{2,1,0:T(8,128)} %get-tuple-element.1126), channel_id=1, source_target_pairs={{0,1},{1,2},{2,3},{3,4},{4,5},{5,6},{6,7},{7,8},{8,9},{9,10},{10,1... | collective-permute-start | bytes 147464 | tf_op jit(solution)/shard_map/ppermute | solution.py:34
  334.2 15.3 %copy-start.78 = (f32[16,256]{1,0:T(8,128)}, f32[16,256]{1,0:T(8,128)S(1)}, u32[]{:S(2)}) copy-start(f32[16,256]{1,0:T(8,128)S(1)} %pad.494) | copy-start | bytes 49156
  389.4 277.2 %all-reduce.104.cloned.1.call-start = ((), (), s32[]{:S(2)}) async-start(), calls=%async_computation.6 | async-start | bytes 131072 | tf_op jit(solution)/shard_map/psum | solution.py:237
  394.0 84.6 %copy-start.15 = (f32[6,16,256]{2,1,0:T(8,128)S(1)}, f32[6,16,256]{2,1,0:T(8,128)}, u32[]{:S(2)}) copy-start(f32[6,16,256]{2,1,0:T(8,128)} %copy-done.13) | copy-start | bytes 294916
  394.0 84.6 %copy-start.73 = (f32[256]{0:T(256)S(1)}, f32[256]{0:T(256)}, u32[]{:S(2)}) copy-start(f32[256]{0:T(256)} %copy-done.71) | copy-start | bytes 3076
  394.0 84.6 %copy-start.79 = (f32[16,256]{1,0:T(8,128)S(1)}, f32[16,256]{1,0:T(8,128)}, u32[]{:S(2)}) copy-start(f32[16,256]{1,0:T(8,128)} %copy-done.78) | copy-start | bytes 49156
  394.0 84.6 %copy-start.80 = (f32[16,256]{1,0:T(8,128)S(1)}, f32[16,256]{1,0:T(8,128)}, u32[]{:S(2)}) copy-start(f32[16,256]{1,0:T(8,128)} %pad.495) | copy-start | bytes 49156
  394.0 84.6 %copy-start.110 = (f32[256]{0:T(256)S(1)}, f32[256]{0:T(256)}, u32[]{:S(2)}) copy-start(f32[256]{0:T(256)} %get-tuple-element.904) | copy-start | bytes 3076
  394.0 84.6 %copy-start.12 = (f32[6,16,256]{2,1,0:T(8,128)S(1)}, f32[6,16,256]{2,1,0:T(8,128)}, u32[]{:S(2)}) copy-start(f32[6,16,256]{2,1,0:T(8,128)} %param.57) | copy-start | bytes 294916
  394.1 83.7 %collective-permute-start.10 = (f32[6,16,128]{2,1,0:T(8,128)S(1)}, f32[6,16,128]{2,1,0:T(8,128)S(1)}, u32[]{:S(2)}, u32[]{:S(2)}) collective-permute-start(f32[6,16,128]{2,1,0:T(8,128)S(1)} %copy-done.104), channel_id=1, source_target_pairs={{0,1},{1,2},{2,3},{3,4},{4,5},{5,6},{6,7},{7,8},{8,9},{9,10},{10,1... | collective-permute-start | bytes 147464 | tf_op jit(solution)/shard_map/ppermute | solution.py:34
  395.7 82.1 %collective-permute-start.11 = (f32[6,16,128]{2,1,0:T(8,128)S(1)}, f32[6,16,128]{2,1,0:T(8,128)S(1)}, u32[]{:S(2)}, u32[]{:S(2)}) collective-permute-start(f32[6,16,128]{2,1,0:T(8,128)S(1)} %copy-done.103), channel_id=1, source_target_pairs={{0,31},{1,0},{2,1},{3,2},{4,3},{5,4},{6,5},{7,6},{8,7},{9,8},{10,9... | collective-permute-start | bytes 147464 | tf_op jit(solution)/shard_map/ppermute | solution.py:34
  (106 other events, 383.8 us)
Sparse Core Ops, SparseCore 0:
  171.0 33.0 reduce-scatter.3
  267.0 31.3 reduce-scatter.5
  389.5 30.6 reduce-scatter.7
  427.1 239.4 all-reduce.103
where the time goes:
time: 680 us; the launch traced here: 675 us
  waiting for transfers between devices  232 us (34%)
  blocking collectives  190 us (28%)
  other arithmetic  85.1 us (13%)
  local copies, waits for them, and re-layouts  63.4 us (9%)
  starting transfers between devices  60.1 us (9%)
  matrix products  26.9 us (4%)
  between operations  16.2 us (2%)
    psum x1, waiting for transfers between devices, on_device(): lax.psum((TIME_STEP * (grads_two[0] + grads_one[0] + grads_zero[0]), TIME...  187 us
    psum x1, blocking collectives, on_device(): lax.psum((TIME_STEP * (grads_two[0] + grads_one[0] + grads_zero[0]), TIME...  73.1 us
    all_gather x7, blocking collectives, prefix(): everything = jax.tree.map(lambda part: lax.all_gather(part, axis), shard)  73 us
    all_gather x3, blocking collectives, heating(): lax.all_gather(theta, 'gz', axis=0, tiled=True)  43.7 us
    select_n x48, other arithmetic, step(): return jax.tree.map(lambda a, b: jnp.where(reached, a, b), new, before)  35.2 us
    ppermute x3, starting transfers between devices, padded_2(): after = lax.ppermute(first, axis, down)  32.3 us
    ppermute x6, starting transfers between devices, passed_along(): lax.ppermute(shard, axis, [(i, (i + by) % length) for i in range(length)])  27.5 us
    reduce_scatter x3, waiting for transfers between devices, heating_adjoint(): lax.psum_scatter(lax.dot_general(own_rows, lead_theta, (((0,), (0,)), (()...  24.4 us
  transfers between devices with their start and end apart: 16, of which 5 were waited for; matrix products, arithmetic and copies ran while one was open for 3% of the time, Pallas kernels for 0%

commit v1 on v0

--- a/solution.py
+++ b/solution.py
@@ -234,14 +234,13 @@
     cot_one = lead_one + TIME_STEP * back_one
     back_zero, grads_zero = section_adjoint(padded_zero, cot_one)
     grad_state = grad_state + cot_one + TIME_STEP * back_zero
-    totals = lax.psum(
-        (
-            TIME_STEP * (grads_two[0] + grads_one[0] + grads_zero[0]),
-            TIME_STEP * (grads_two[1] + grads_one[1] + grads_zero[1]),
-            TIME_STEP * (grads_two[2] + grads_one[2] + grads_zero[2]),
-        ),
-        ("gz", "gx"),
-    )
+    totals = (
+        TIME_STEP * (grads_two[0] + grads_one[0] + grads_zero[0]),
+        TIME_STEP * (grads_two[1] + grads_one[1] + grads_zero[1]),
+        TIME_STEP * (grads_two[2] + grads_one[2] + grads_zero[2]),
+    )
+    for over in ("gz", "gx"):
+        totals = lax.psum(totals, over)
     return (new_state, grad_state, totals[0], totals[1], totals[2])
 
 

time: 680 us -> 999 us (1.47)
  waiting for transfers between devices: 232 us -> 440 us
  blocking collectives: 190 us -> 336 us
  other arithmetic: 85.1 us -> 56 us
    psum x1 -> x2, waiting for transfers between devices: 187 us -> 395 us  [on_device(): totals = lax.psum(totals, over)]
    psum x1 -> x2, blocking collectives: 73.1 us -> 220 us  [on_device(): totals = lax.psum(totals, over)]
    select_n x48, other arithmetic: 35.2 us -> 18.6 us  [step(): return jax.tree.map(lambda a, b: jnp.where(reached, a, b), new, before)]
  transfers between devices with their start and end apart: 16 -> 17, of which waited for: 5 -> 5; matrix products, arithmetic and copies ran while one was open for 3% -> 2% of each run, Pallas kernels for 0% -> 0%
where the time goes in v1:
time: 999 us; the launch traced here: 986 us
  waiting for transfers between devices  440 us (44%)
  blocking collectives  336 us (34%)
  starting transfers between devices  57.2 us (6%)
  other arithmetic  56 us (6%)
  local copies, waits for them, and re-layouts  53.6 us (5%)
  matrix products  25.1 us (3%)
  between operations  16.3 us (2%)
    psum x2, waiting for transfers between devices, on_device(): totals = lax.psum(totals, over)  395 us
    psum x2, blocking collectives, on_device(): totals = lax.psum(totals, over)  220 us
    all_gather x7, blocking collectives, prefix(): everything = jax.tree.map(lambda part: lax.all_gather(part, axis), shard)  73 us
    all_gather x3, blocking collectives, heating(): lax.all_gather(theta, 'gz', axis=0, tiled=True)  43.7 us
    ppermute x3, starting transfers between devices, padded_2(): after = lax.ppermute(first, axis, down)  32.3 us
    ppermute x6, starting transfers between devices, passed_along(): lax.ppermute(shard, axis, [(i, (i + by) % length) for i in range(length)])  24.8 us
    reduce_scatter x3, waiting for transfers between devices, heating_adjoint(): lax.psum_scatter(lax.dot_general(own_rows, lead_theta, (((0,), (0,)), (()...  24.4 us
    ppermute x6, waiting for transfers between devices, passed_along(): lax.ppermute(shard, axis, [(i, (i + by) % length) for i in range(length)])  21.4 us
  transfers between devices with their start and end apart: 17, of which 5 were waited for; matrix products, arithmetic and copies ran while one was open for 2% of the time, Pallas kernels for 0%

profile of v1, /device:TPU:1, one launch (start us, length us, event | category | flops | bytes accessed | tf_op | source)
XLA Modules:
  0.0 986.0 jit_solution(12080212071347931494)
XLA Ops:
  8.1 12.5 %collective-permute-start = (f32[6,16,128]{2,1,0:T(8,128)S(1)}, f32[6,16,128]{2,1,0:T(8,128)S(1)}, u32[]{:S(2)}, u32[]{:S(2)}) collective-permute-start(f32[6,16,128]{2,1,0:T(8,128)S(1)} %get-tuple-element.1232), channel_id=1, source_target_pairs={{1,0},{2,1},{3,2},{4,3},{5,4},{6,5},{7,6},{8,7},{9,8},{10,9},{11,1... | collective-permute-start | bytes 147464 | tf_op jit(solution)/shard_map/ppermute | solution.py:45
  21.9 1.4 bitcast_multiply_fusion
  23.7 1.5 fusion.147
  25.2 1.5 fusion.146
  27.8 1.6 fusion.145
  30.5 11.1 %all-gather.3 = f32[8,1,256]{2,1,0:T(1,128)S(1)} all-gather(f32[1,1,256]{2,1,0:T(1,128)S(1)} %add_bitcast_fusion.6), channel_id=1, replica_groups=mesh['gz'=8,'gx'=32] {'gz'}, dimensions={0}, use_global_device_ids=true | all-gather | bytes 9216 | tf_op jit(solution)/shard_map/all_gather | solution.py:16
  41.6 8.7 all-gather.4
  51.5 14.0 %all-gather = f32[1,128,256]{2,1,0:T(8,128)S(1)} all-gather(f32[1,16,256]{2,1,0:T(8,128)S(1)} %slice-done), channel_id=2, replica_groups=mesh['gz'=8,'gx'=32] {'gz'}, dimensions={1}, use_global_device_ids=true | all-gather | bytes 147456 | tf_op jit(solution)/shard_map/all_gather | solution.py:146
  73.2 10.1 %all-gather.5 = f32[8,1,256]{2,1,0:T(1,128)S(1)} all-gather(f32[1,1,256]{2,1,0:T(1,128)S(1)} %add_bitcast_fusion.4), channel_id=1, replica_groups=mesh['gz'=8,'gx'=32] {'gz'}, dimensions={0}, use_global_device_ids=true | all-gather | bytes 9216 | tf_op jit(solution)/shard_map/all_gather | solution.py:16
  84.4 9.9 collective-permute-start.2
  94.3 14.3 %all-gather.1 = f32[1,128,256]{2,1,0:T(8,128)S(1)} all-gather(f32[1,16,256]{2,1,0:T(8,128)S(1)} %get-tuple-element.1174), channel_id=3, replica_groups=mesh['gz'=8,'gx'=32] {'gz'}, dimensions={1}, use_global_device_ids=true | all-gather | bytes 147456 | tf_op jit(solution)/shard_map/all_gather | solution.py:146
  113.2 9.9 %collective-permute-start.4 = (f32[6,16,128]{2,1,0:T(8,128)S(1)}, f32[6,16,128]{2,1,0:T(8,128)S(1)}, u32[]{:S(2)}, u32[]{:S(2)}) collective-permute-start(f32[6,16,128]{2,1,0:T(8,128)S(1)} %get-tuple-element.1195), channel_id=1, source_target_pairs={{1,0},{2,1},{3,2},{4,3},{5,4},{6,5},{7,6},{8,7},{9,8},{10,9},{11,1... | collective-permute-start | bytes 147464 | tf_op jit(solution)/shard_map/ppermute | solution.py:45
  123.2 15.5 %all-gather.2 = f32[1,128,256]{2,1,0:T(8,128)} all-gather(f32[1,16,256]{2,1,0:T(8,128)S(1)} %get-tuple-element.1190), channel_id=4, replica_groups=mesh['gz'=8,'gx'=32] {'gz'}, dimensions={1}, use_global_device_ids=true | all-gather | bytes 147456 | tf_op jit(solution)/shard_map/all_gather | solution.py:146
  138.7 1.5 broadcast_multiply_fusion
  153.4 8.7 all-gather.7
  162.2 9.5 while.111
  162.8 1.3 add_select_fusion.15
  164.1 1.3 add_select_fusion.15
  165.3 1.3 add_select_fusion.15
  166.6 1.3 add_select_fusion.15
  167.9 1.3 add_select_fusion.15
  171.7 9.9 %collective-permute-start.7 = (f32[6,16,128]{2,1,0:T(8,128)S(1)}, f32[6,16,128]{2,1,0:T(8,128)S(1)}, u32[]{:S(2)}, u32[]{:S(2)}) collective-permute-start(f32[6,16,128]{2,1,0:T(8,128)S(1)} %get-tuple-element.1129), channel_id=1, source_target_pairs={{0,31},{1,0},{2,1},{3,2},{4,3},{5,4},{6,5},{7,6},{8,7},{9,8},{10,9... | collective-permute-start | bytes 147464 | tf_op jit(solution)/shard_map/ppermute | solution.py:34
  181.7 11.1 %collective-permute-done.6 = f32[6,16,128]{2,1,0:T(8,128)S(1)} collective-permute-done((f32[6,16,128]{2,1,0:T(8,128)S(1)}, f32[6,16,128]{2,1,0:T(8,128)S(1)}, u32[]{:S(2)}, u32[]{:S(2)}) %collective-permute-start.6) | collective-permute-done | bytes 49184 | tf_op jit(solution)/shard_map/ppermute | solution.py:34
  192.8 12.0 %reduce-scatter.4.cloned.1.call-done = f32[16,256]{1,0:T(8,128)} async-done(((f32[128,256]{1,0:T(8,128)}), f32[16,256]{1,0:T(8,128)}) %reduce-scatter.4.cloned.1.call-update) | async-done | bytes 16400 | tf_op jit(solution)/shard_map/reduce_scatter | solution.py:155
  211.8 2.2 fusion.2
  219.0 1.9 pad.467
  220.9 1.9 pad.468
  222.8 1.3 add.1088
  226.0 1.9 pad.470
  227.9 1.3 add.1090
  231.2 1.9 pad.472
  233.9 12.0 %all-gather.8 = f32[8,1,256]{2,1,0:T(1,128)S(1)} all-gather(f32[1,1,256]{2,1,0:T(1,128)S(1)} %add_bitcast_fusion.1), channel_id=1, replica_groups=mesh['gz'=8,'gx'=32] {'gz'}, dimensions={0}, use_global_device_ids=true | all-gather | bytes 9216 | tf_op jit(solution)/shard_map/all_gather | solution.py:16
  246.5 14.5 %while.112 = (s32[]{:T(128)}, f32[256]{0:T(256)}, s32[]{:T(128)}, f32[8,256]{1,0:T(8,128)}, f32[8,256]{1,0:T(8,128)}, /*index=5*/s32[]{:T(128)}, s32[]{:T(128)}) while((s32[]{:T(128)}, f32[256]{0:T(256)}, s32[]{:T(128)}, f32[8,256]{1,0:T(8,128)}, f32[8,256]{1,0:T(8,128)}, /*index=5*/s32[]{:T(128)}, s32[]{:T(128)}) %tuple.461), condition=%wide.region_15.16_spmd.clone, body=%wide.region_14.15_spmd.clone.sunk | while | flops 1028 | bytes 8301 | solution.py:29
  261.0 2.6 convolution_add_fusion.5
  263.6 2.4 convolution_add_fusion.1
  267.0 7.8 collective-permute-start.9
  275.8 10.3 %collective-permute-done.8 = f32[6,16,128]{2,1,0:T(8,128)S(1)} collective-permute-done((f32[6,16,128]{2,1,0:T(8,128)}, f32[6,16,128]{2,1,0:T(8,128)S(1)}, u32[]{:S(2)}, u32[]{:S(2)}) %collective-permute-start.8) | collective-permute-done | bytes 49184 | tf_op jit(solution)/shard_map/ppermute | solution.py:34
  286.2 12.4 %reduce-scatter.6.cloned.1.call-done = f32[16,256]{1,0:T(8,128)} async-done(((f32[128,256]{1,0:T(8,128)}), f32[16,256]{1,0:T(8,128)}) %reduce-scatter.6.cloned.1.call-update) | async-done | bytes 16400 | tf_op jit(solution)/shard_map/reduce_scatter | solution.py:155
  300.0 1.7 multiply_reduce_fusion.1
  312.3 12.0 %all-gather.9 = f32[8,1,256]{2,1,0:T(1,128)S(1)} all-gather(f32[1,1,256]{2,1,0:T(1,128)S(1)} %add_bitcast_fusion), channel_id=1, replica_groups=mesh['gz'=8,'gx'=32] {'gz'}, dimensions={0}, use_global_device_ids=true | all-gather | bytes 9216 | tf_op jit(solution)/shard_map/all_gather | solution.py:16
  324.4 5.9 while.113
  330.3 10.4 %all-gather.6 = f32[8,1,256]{2,1,0:T(1,128)S(1)} all-gather(f32[1,1,256]{2,1,0:T(1,128)S(1)} %add_bitcast_fusion.3), channel_id=1, replica_groups=mesh['gz'=8,'gx'=32] {'gz'}, dimensions={0}, use_global_device_ids=true | all-gather | bytes 9216 | tf_op jit(solution)/shard_map/all_gather | solution.py:16
  340.7 5.9 while.110
  353.7 7.0 collective-permute-start.11
  361.4 22.8 %all-reduce.102 = (f32[128,12]{0,1:T(8,128)S(1)}, f32[6,128]{1,0:T(8,128)S(1)}) all-reduce(f32[128,12]{0,1:T(8,128)S(1)} %copy-done.108, f32[6,128]{1,0:T(8,128)S(1)} %copy-done.120), channel_id=1, replica_groups=mesh['gz'=8,'gx'=32] {'gz'}, use_global_device_ids=true, to_apply=%region_21.22 | all-reduce | flops 2304 | bytes 18432 | tf_op jit(solution)/shard_map/psum | solution.py:243
  384.2 196.8 %all-reduce.101 = (f32[128,12]{0,1:T(8,128)}, f32[6,128]{1,0:T(8,128)}) all-reduce(f32[128,12]{0,1:T(8,128)S(1)} %get-tuple-element.1081, f32[6,128]{1,0:T(8,128)S(1)} %get-tuple-element.1082), channel_id=1, replica_groups=mesh['gz'=8,'gx'=32] {'gx'}, use_global_device_ids=true, to_apply=%region_22.23 | all-reduce | flops 2304 | bytes 18432 | tf_op jit(solution)/shard_map/psum | solution.py:243
  583.3 394.6 %all-reduce.108.cloned.1.call-done = f32[128,128]{1,0:T(8,128)} async-done(((f32[128,128]{1,0:T(8,128)}), f32[128,128]{1,0:T(8,128)}) %all-reduce.108.cloned.1.call-update) | async-done | bytes 65552 | tf_op jit(solution)/shard_map/psum | solution.py:243
  978.0 1.5 copy.128
  (713 shorter events, 101.7 us)
Async XLA Ops:
  7.2 62.3 %copy-start = (f32[128,128]{1,0:T(8,128)S(1)}, f32[128,128]{1,0:T(8,128)}, u32[]{:S(2)}) copy-start(f32[128,128]{1,0:T(8,128)} %param.61) | copy-start | bytes 196612
  7.2 44.3 %slice-start = ((f32[6,16,256]{2,1,0:T(8,128)}), f32[1,16,256]{2,1,0:T(8,128)S(1)}, s32[]{:S(2)}) async-start(f32[6,16,256]{2,1,0:T(8,128)} %param.56), calls=%async_computation.8 | async-start | bytes 32768 | tf_op jit(solution)/shard_map/slice | solution.py:180
  7.2 58.3 %copy-start.7 = (f32[6,16,256]{2,1,0:T(8,128)S(1)}, f32[6,16,256]{2,1,0:T(8,128)}, u32[]{:S(2)}) copy-start(f32[6,16,256]{2,1,0:T(8,128)} %param.56) | copy-start | bytes 294916
  7.2 58.5 %copy-start.57 = (bf16[128,12]{0,1:T(8,128)(2,1)S(1)}, bf16[128,12]{0,1:T(8,128)(2,1)}, u32[]{:S(2)}) copy-start(bf16[128,12]{0,1:T(8,128)(2,1)} %param.58) | copy-start | bytes 9220
  7.2 197.6 %reduce-scatter.4.cloned.1.call-start = ((), (), s32[]{:S(2)}) async-start(), calls=%async_computation.3 | async-start | bytes 147456 | tf_op jit(solution)/shard_map/reduce_scatter | solution.py:155
  8.1 57.4 %collective-permute-start = (f32[6,16,128]{2,1,0:T(8,128)S(1)}, f32[6,16,128]{2,1,0:T(8,128)S(1)}, u32[]{:S(2)}, u32[]{:S(2)}) collective-permute-start(f32[6,16,128]{2,1,0:T(8,128)S(1)} %get-tuple-element.1232), channel_id=1, source_target_pairs={{1,0},{2,1},{3,2},{4,3},{5,4},{6,5},{7,6},{8,7},{9,8},{10,9},{11,1... | collective-permute-start | bytes 147464 | tf_op jit(solution)/shard_map/ppermute | solution.py:45
  20.6 44.9 %collective-permute-start.1 = (f32[6,16,128]{2,1,0:T(8,128)S(1)}, f32[6,16,128]{2,1,0:T(8,128)S(1)}, u32[]{:S(2)}, u32[]{:S(2)}) collective-permute-start(f32[6,16,128]{2,1,0:T(8,128)S(1)} %get-tuple-element.1233), channel_id=1, source_target_pairs={{0,1},{1,2},{2,3},{3,4},{4,5},{5,6},{6,7},{7,8},{8,9},{9,10},{10,1... | collective-permute-start | bytes 147464 | tf_op jit(solution)/shard_map/ppermute | solution.py:44
  21.9 119.6 %copy-start.60 = (f32[256]{0:T(256)}, f32[256]{0:T(256)S(1)}, u32[]{:S(2)}) copy-start(f32[256]{0:T(256)S(1)} %get-tuple-element.1106) | copy-start | bytes 3076
  21.9 130.8 %copy-start.54 = (f32[256]{0:T(256)}, f32[256]{0:T(256)S(1)}, u32[]{:S(2)}) copy-start(f32[256]{0:T(256)S(1)} %get-tuple-element.1107) | copy-start | bytes 3076
  23.4 118.3 %copy-start.41 = (f32[256]{0:T(256)}, f32[256]{0:T(256)S(1)}, u32[]{:S(2)}) copy-start(f32[256]{0:T(256)S(1)} %get-tuple-element.1277) | copy-start | bytes 3076
  30.1 110.1 %copy-start.65 = (f32[256]{0:T(256)}, f32[256]{0:T(256)S(1)}, u32[]{:S(2)}) copy-start(f32[256]{0:T(256)S(1)} %convert_element_type.59) | copy-start | bytes 3076
  50.8 154.7 %copy-start.26 = (f32[16,256]{1,0:T(8,128)}, f32[16,256]{1,0:T(8,128)S(1)}, u32[]{:S(2)}) copy-start(f32[16,256]{1,0:T(8,128)S(1)} %get-tuple-element.1105) | copy-start | bytes 49156
  73.0 36.8 %copy-start.21 = (bf16[1,6,16,256]{3,1,2,0:T(8,128)(2,1)}, bf16[1,6,16,256]{3,1,2,0:T(8,128)(2,1)S(1)}, u32[]{:S(2)}) copy-start(bf16[1,6,16,256]{3,1,2,0:T(8,128)(2,1)S(1)} %copy.23) | copy-start | bytes 147460
  84.4 24.1 %collective-permute-start.2 = (f32[6,16,128]{2,1,0:T(8,128)S(1)}, f32[6,16,128]{2,1,0:T(8,128)S(1)}, u32[]{:S(2)}, u32[]{:S(2)}) collective-permute-start(f32[6,16,128]{2,1,0:T(8,128)S(1)} %get-tuple-element.1216), channel_id=1, source_target_pairs={{1,0},{2,1},{3,2},{4,3},{5,4},{6,5},{7,6},{8,7},{9,8},{10,9},{11,1... | collective-permute-start | bytes 147464 | tf_op jit(solution)/shard_map/ppermute | solution.py:45
  94.3 14.3 %collective-permute-start.3 = (f32[6,16,128]{2,1,0:T(8,128)S(1)}, f32[6,16,128]{2,1,0:T(8,128)S(1)}, u32[]{:S(2)}, u32[]{:S(2)}) collective-permute-start(f32[6,16,128]{2,1,0:T(8,128)S(1)} %get-tuple-element.1217), channel_id=1, source_target_pairs={{0,1},{1,2},{2,3},{3,4},{4,5},{5,6},{6,7},{7,8},{8,9},{9,10},{10,1... | collective-permute-start | bytes 147464 | tf_op jit(solution)/shard_map/ppermute | solution.py:44
  113.2 25.4 %collective-permute-start.4 = (f32[6,16,128]{2,1,0:T(8,128)S(1)}, f32[6,16,128]{2,1,0:T(8,128)S(1)}, u32[]{:S(2)}, u32[]{:S(2)}) collective-permute-start(f32[6,16,128]{2,1,0:T(8,128)S(1)} %get-tuple-element.1195), channel_id=1, source_target_pairs={{1,0},{2,1},{3,2},{4,3},{5,4},{6,5},{7,6},{8,7},{9,8},{10,9},{11,1... | collective-permute-start | bytes 147464 | tf_op jit(solution)/shard_map/ppermute | solution.py:45
  123.2 15.5 %collective-permute-start.5 = (f32[6,16,128]{2,1,0:T(8,128)S(1)}, f32[6,16,128]{2,1,0:T(8,128)S(1)}, u32[]{:S(2)}, u32[]{:S(2)}) collective-permute-start(f32[6,16,128]{2,1,0:T(8,128)S(1)} %get-tuple-element.1196), channel_id=1, source_target_pairs={{0,1},{1,2},{2,3},{3,4},{4,5},{5,6},{6,7},{7,8},{8,9},{9,10},{10,1... | collective-permute-start | bytes 147464 | tf_op jit(solution)/shard_map/ppermute | solution.py:44
  150.5 55.1 %copy-start.66 = (f32[256]{0:T(256)S(1)}, f32[256]{0:T(256)}, u32[]{:S(2)}) copy-start(f32[256]{0:T(256)} %copy-done.65) | copy-start | bytes 3076
  150.7 58.2 %copy-start.42 = (f32[256]{0:T(256)S(1)}, f32[256]{0:T(256)}, u32[]{:S(2)}) copy-start(f32[256]{0:T(256)} %copy-done.41) | copy-start | bytes 3076
  150.9 58.1 %copy-start.89 = (f32[256]{0:T(256)S(1)}, f32[256]{0:T(256)}, u32[]{:S(2)}) copy-start(f32[256]{0:T(256)} %copy-done.86) | copy-start | bytes 3076
  150.9 60.9 %copy-start.69 = (bf16[6,128]{1,0:T(8,128)(2,1)S(1)}, bf16[6,128]{1,0:T(8,128)(2,1)}, u32[]{:S(2)}) copy-start(bf16[6,128]{1,0:T(8,128)(2,1)} %param.60) | copy-start | bytes 4612
  171.7 126.9 %reduce-scatter.6.cloned.1.call-start = ((), (), s32[]{:S(2)}) async-start(), calls=%async_computation.4 | async-start | bytes 147456 | tf_op jit(solution)/shard_map/reduce_scatter | solution.py:155
  171.7 21.1 %collective-permute-start.7 = (f32[6,16,128]{2,1,0:T(8,128)S(1)}, f32[6,16,128]{2,1,0:T(8,128)S(1)}, u32[]{:S(2)}, u32[]{:S(2)}) collective-permute-start(f32[6,16,128]{2,1,0:T(8,128)S(1)} %get-tuple-element.1129), channel_id=1, source_target_pairs={{0,31},{1,0},{2,1},{3,2},{4,3},{5,4},{6,5},{7,6},{8,7},{9,8},{10,9... | collective-permute-start | bytes 147464 | tf_op jit(solution)/shard_map/ppermute | solution.py:34
  181.7 11.1 %collective-permute-start.6 = (f32[6,16,128]{2,1,0:T(8,128)S(1)}, f32[6,16,128]{2,1,0:T(8,128)S(1)}, u32[]{:S(2)}, u32[]{:S(2)}) collective-permute-start(f32[6,16,128]{2,1,0:T(8,128)S(1)} %get-tuple-element.1130), channel_id=1, source_target_pairs={{0,1},{1,2},{2,3},{3,4},{4,5},{5,6},{6,7},{7,8},{8,9},{9,10},{10,1... | collective-permute-start | bytes 147464 | tf_op jit(solution)/shard_map/ppermute | solution.py:34
  263.6 35.6 %copy-start.27 = (f32[16,256]{1,0:T(8,128)S(1)}, f32[16,256]{1,0:T(8,128)}, u32[]{:S(2)}) copy-start(f32[16,256]{1,0:T(8,128)} %copy-done.26) | copy-start | bytes 49156
  266.9 42.2 %copy-start.91 = (f32[16,256]{1,0:T(8,128)S(1)}, f32[16,256]{1,0:T(8,128)}, u32[]{:S(2)}) copy-start(f32[16,256]{1,0:T(8,128)} %get-tuple-element.1164) | copy-start | bytes 49156
  266.9 42.2 %copy-start.113 = (pred[256]{0:T(512)(128)(4,1)S(1)}, pred[256]{0:T(512)(128)(4,1)}, u32[]{:S(2)}) copy-start(pred[256]{0:T(512)(128)(4,1)} %get-tuple-element.1280) | copy-start | bytes 772
  266.9 42.2 %copy-start.118 = (pred[256]{0:T(512)(128)(4,1)S(1)}, pred[256]{0:T(512)(128)(4,1)}, u32[]{:S(2)}) copy-start(pred[256]{0:T(512)(128)(4,1)} %get-tuple-element.1281) | copy-start | bytes 772
  266.9 45.2 %copy-start.62 = (f32[256]{0:T(256)S(1)}, f32[256]{0:T(256)}, u32[]{:S(2)}) copy-start(f32[256]{0:T(256)} %copy-done.60) | copy-start | bytes 3076
  266.9 45.3 %copy-start.56 = (f32[256]{0:T(256)S(1)}, f32[256]{0:T(256)}, u32[]{:S(2)}) copy-start(f32[256]{0:T(256)} %copy-done.54) | copy-start | bytes 3076
  266.9 57.5 %copy-start.103 = (f32[256]{0:T(256)S(1)}, f32[256]{0:T(256)}, u32[]{:S(2)}) copy-start(f32[256]{0:T(256)} %custom-call.5) | copy-start | bytes 3076
  266.9 73.8 %copy-start.101 = (f32[256]{0:T(256)S(1)}, f32[256]{0:T(256)}, u32[]{:S(2)}) copy-start(f32[256]{0:T(256)} %custom-call.2) | copy-start | bytes 3076
  266.9 314.2 %all-reduce.106.cloned.1.call-start = ((), (), s32[]{:S(2)}) async-start(), calls=%async_computation.6 | async-start | bytes 131072 | tf_op jit(solution)/shard_map/psum | solution.py:243
  267.0 19.2 %collective-permute-start.9 = (f32[6,16,128]{2,1,0:T(8,128)}, f32[6,16,128]{2,1,0:T(8,128)S(1)}, u32[]{:S(2)}, u32[]{:S(2)}) collective-permute-start(f32[6,16,128]{2,1,0:T(8,128)} %get-tuple-element.1127), channel_id=1, source_target_pairs={{0,31},{1,0},{2,1},{3,2},{4,3},{5,4},{6,5},{7,6},{8,7},{9,8},{10,9... | collective-permute-start | bytes 147464 | tf_op jit(solution)/shard_map/ppermute | solution.py:34
  274.8 11.3 %collective-permute-start.8 = (f32[6,16,128]{2,1,0:T(8,128)}, f32[6,16,128]{2,1,0:T(8,128)S(1)}, u32[]{:S(2)}, u32[]{:S(2)}) collective-permute-start(f32[6,16,128]{2,1,0:T(8,128)} %get-tuple-element.1128), channel_id=1, source_target_pairs={{0,1},{1,2},{2,3},{3,4},{4,5},{5,6},{6,7},{7,8},{8,9},{9,10},{10,1... | collective-permute-start | bytes 147464 | tf_op jit(solution)/shard_map/ppermute | solution.py:34
  275.8 71.5 %copy-start.70 = (bf16[6,128]{1,0:T(8,128)(2,1)S(1)}, bf16[6,128]{1,0:T(8,128)(2,1)}, u32[]{:S(2)}) copy-start(bf16[6,128]{1,0:T(8,128)(2,1)} %param.60) | copy-start | bytes 4612
  312.2 35.7 %copy-start.119 = (f32[6,128]{1,0:T(8,128)S(1)}, f32[6,128]{1,0:T(8,128)}, u32[]{:S(2)}) copy-start(f32[6,128]{1,0:T(8,128)} %convolution_add_fusion.5) | copy-start | bytes 9220
  312.3 35.0 %copy-start.74 = (f32[16,256]{1,0:T(8,128)}, f32[16,256]{1,0:T(8,128)S(1)}, u32[]{:S(2)}) copy-start(f32[16,256]{1,0:T(8,128)S(1)} %pad.495) | copy-start | bytes 49156
  352.3 228.9 %reduce-scatter.8.cloned.1.call-start = ((), (), s32[]{:S(2)}) async-start(), calls=%async_computation.5 | async-start | bytes 147456 | tf_op jit(solution)/shard_map/reduce_scatter | solution.py:155
  352.5 229.4 %copy-start.67 = (f32[256]{0:T(256)S(1)}, f32[256]{0:T(256)}, u32[]{:S(2)}) copy-start(f32[256]{0:T(256)} %copy-done.65) | copy-start | bytes 3076
  352.5 229.4 %copy-start.73 = (f32[16,256]{1,0:T(8,128)S(1)}, f32[16,256]{1,0:T(8,128)}, u32[]{:S(2)}) copy-start(f32[16,256]{1,0:T(8,128)} %copy-done.72) | copy-start | bytes 49156
  352.5 229.4 %copy-start.75 = (f32[16,256]{1,0:T(8,128)S(1)}, f32[16,256]{1,0:T(8,128)}, u32[]{:S(2)}) copy-start(f32[16,256]{1,0:T(8,128)} %copy-done.74) | copy-start | bytes 49156
  352.6 229.4 %copy-start.94 = (f32[16,256]{1,0:T(8,128)S(1)}, f32[16,256]{1,0:T(8,128)}, u32[]{:S(2)}) copy-start(f32[16,256]{1,0:T(8,128)} %rev.15) | copy-start | bytes 49156
  352.6 229.4 %copy-start.105 = (f32[256]{0:T(256)S(1)}, f32[256]{0:T(256)}, u32[]{:S(2)}) copy-start(f32[256]{0:T(256)} %copy-done.104) | copy-start | bytes 3076
  352.6 229.4 %copy-start.10 = (f32[6,16,256]{2,1,0:T(8,128)S(1)}, f32[6,16,256]{2,1,0:T(8,128)}, u32[]{:S(2)}) copy-start(f32[6,16,256]{2,1,0:T(8,128)} %param.57) | copy-start | bytes 294916
  353.7 227.4 %collective-permute-start.11 = (f32[6,16,128]{2,1,0:T(8,128)S(1)}, f32[6,16,128]{2,1,0:T(8,128)S(1)}, u32[]{:S(2)}, u32[]{:S(2)}) collective-permute-start(f32[6,16,128]{2,1,0:T(8,128)S(1)} %get-tuple-element.1125), channel_id=1, source_target_pairs={{0,31},{1,0},{2,1},{3,2},{4,3},{5,4},{6,5},{7,6},{8,7},{9,8},{10,9... | collective-permute-start | bytes 147464 | tf_op jit(solution)/shard_map/ppermute | solution.py:34
  360.7 220.4 %collective-permute-start.10 = (f32[6,16,128]{2,1,0:T(8,128)S(1)}, f32[6,16,128]{2,1,0:T(8,128)S(1)}, u32[]{:S(2)}, u32[]{:S(2)}) collective-permute-start(f32[6,16,128]{2,1,0:T(8,128)S(1)} %get-tuple-element.1126), channel_id=1, source_target_pairs={{0,1},{1,2},{2,3},{3,4},{4,5},{5,6},{6,7},{7,8},{8,9},{9,10},{10,1... | collective-permute-start | bytes 147464 | tf_op jit(solution)/shard_map/ppermute | solution.py:34
  361.3 616.7 %all-reduce.108.cloned.1.call-start = ((), (), s32[]{:S(2)}) async-start(), calls=%async_computation.7 | async-start | bytes 131072 | tf_op jit(solution)/shard_map/psum | solution.py:243
  (99 other events, 489.4 us)
Sparse Core Ops, SparseCore 0:
  171.8 33.0 reduce-scatter.3
  267.1 31.4 reduce-scatter.5
  352.4 64.7 all-reduce.105
  419.7 33.8 reduce-scatter.7
  581.3 396.6 all-reduce.107
